TPU v7x, 32 devices: a whole 2x2x4 slice. The times are simulated.
32 devices in a mesh: island: 2 (over x), row: 4 (over y, core), col: 4 (over z).
Axes of the slice: x: 2, y: 2, z: 4, core: 2. Of those that a mesh axis runs over, the one named last changes fastest.
Arguments:
- deltas: float32 [2, 4096, 8192], P('island', 'row', 'col'), may hold values from -0.13258252 to 0.13258252
- left_stat: float32 [4096, 4096], P(('island', 'col'), 'row'), may hold values from -1.5 to 1.5
- right_stat: float32 [8192, 8192], P(('island', 'row'), 'col'), may hold values from -1.5 to 1.5
Outputs:
- left_new: float32 [4096, 4096], P(('island', 'col'), 'row')
- right_new: float32 [8192, 8192], P(('island', 'row'), 'col')
All inputs are finite; a program needn't handle non-finite values.
Results may differ from a plain program's by a relative error of at most 0.00037.
Values may be sent and summed in bfloat16 or wider, within the bound.
A program may use at most 128 MiB of HBM per device.

v0:
```python
import jax
import jax.numpy as jnp
from jax import lax
from jax.sharding import PartitionSpec as P

M = 4096
N = 8192


def broadcast(value, axis, source):
    kept = jnp.where(lax.axis_index(axis) == source, value, 0).astype(value.dtype)
    return lax.psum(kept, axis)


def local(deltas, left_stat, right_stat):
    islands = lax.axis_size("island")
    row_count = lax.axis_size("row")
    island = lax.axis_index("island")
    local_delta = deltas[0]
    shares = lax.psum_scatter(local_delta, "island", scatter_dimension=0, tiled=True)
    rounded = (shares / islands).astype(jnp.bfloat16)
    panel = lax.all_gather(rounded, "island", axis=0, tiled=True)
    rows_local = panel.shape[0]
    rows_island = M // islands
    row_pieces = max(1, row_count // islands)
    row_extent = min(rows_island, rows_local)
    blocks = []
    for number in range(row_pieces):
        start_row = island * rows_island + number * row_extent
        source = start_row // rows_local
        blocks.append(broadcast(panel, "row", source))
    left_block = jnp.concatenate(blocks, axis=0)
    left_tile = lax.dot_general(
        left_block, panel, (((1,), (1,)), ((), ())), preferred_element_type=jnp.float32
    )
    left_shares = lax.psum_scatter(left_tile, "col", scatter_dimension=0, tiled=True)
    left_new = left_stat + left_shares
    cols_island = N // islands
    whole_rows = lax.all_gather(panel, "col", axis=1, tiled=True)
    right_block = lax.dynamic_slice_in_dim(whole_rows, island * cols_island, cols_island, 1)
    right_tile = lax.dot_general(
        right_block, panel, (((0,), (0,)), ((), ())), preferred_element_type=jnp.float32
    )
    right_shares = lax.psum_scatter(right_tile, "row", scatter_dimension=0, tiled=True)
    right_new = right_stat + right_shares
    return (left_new, right_new)


def solution(mesh):
    in_specs = (P("island", "row", "col"), P(("island", "col"), "row"), P(("island", "row"), "col"))
    out_specs = (P(("island", "col"), "row"), P(("island", "row"), "col"))
    return jax.shard_map(local, mesh=mesh, in_specs=in_specs, out_specs=out_specs, check_vma=False)
```

profile of v0, /device:TPU:0, one launch (start us, length us, event | category | flops | bytes accessed | tf_op | source)
XLA Modules:
  0.0 1020.4 jit_solution(15273571212736628576)
XLA Ops:
  7.2 0.0 reduce-scatter.4.cloned.1.call-start
  7.2 0.7 reduce-scatter.4.cloned.1.call-update
  7.9 0.0 all-gather.3.cloned.1.call-start
  7.9 104.4 %reduce-scatter.4.cloned.1.call-done = f32[512,2048]{1,0:T(8,128)} async-done(((f32[1024,2048]{1,0:T(8,128)}), f32[512,2048]{1,0:T(8,128)}) %reduce-scatter.4.cloned.1.call-update) | async-done | bytes 4194320 | tf_op jit(solution)/shard_map/reduce_scatter | solution.py:20
  112.3 4.0 multiply_convert_fusion
  116.3 0.0 all-gather.3.cloned.1.call-update
  116.4 0.0 all-reduce.3.cloned.1.call-start
  116.4 56.8 %all-gather.3.cloned.1.call-done = bf16[1024,2048]{1,0:T(8,128)(2,1)} async-done(((bf16[512,2048]{1,0:T(8,128)(2,1)}), bf16[1024,2048]{1,0:T(8,128)(2,1)}) %all-gather.3.cloned.1.call-update) | async-done | bytes 4194320 | tf_op jit(solution)/shard_map/all_gather | solution.py:22
  173.2 6.1 broadcast_select_fusion.1
  179.3 0.0 all-reduce.3.cloned.1.call-update
  179.4 0.0 all-gather.5.cloned.1.call-start
  179.4 0.5 all-gather.5.cloned.1.call-update
  179.9 0.0 reduce-scatter.6.cloned.1.call-start
  180.0 152.4 %all-reduce.3.cloned.1.call-done = (bf16[1024,2048]{1,0:T(8,128)(2,1)}, bf16[1024,2048]{1,0:T(8,128)(2,1)}) async-done(((bf16[1024,2048]{1,0:T(8,128)(2,1)}, bf16[1024,2048]{1,0:T(8,128)(2,1)}), (bf16[1024,2048]{1,0:T(8,128)(2,1)}, bf16[1024,2048]{1,0:T(8,128)(2,1)})) %all-reduce.3.cloned.1.call-update) | async-done | bytes 8388624 | tf_op jit(solution)/shard_map/psum | solution.py:12
  332.4 15.2 %fusion = f32[2048,1024]{1,0:T(8,128)} fusion(bf16[1024,2048]{1,0:T(8,128)(2,1)} %all-gather.3.cloned.1.call-done, bf16[1024,2048]{1,0:T(8,128)(2,1)} %get-tuple-element.2, bf16[1024,2048]{1,0:T(8,128)(2,1)} %get-tuple-element.3), kind=kOutput, calls=%fused_computation | convolution fusion | flops 8606711808 | bytes 20971520 | tf_op jit(solution)/shard_map/dot_general | solution.py:33
  347.6 0.0 reduce-scatter.6.cloned.1.call-update
  347.6 0.2 reduce-scatter.8.cloned.1.call-start
  347.9 272.9 %all-gather.5.cloned.1.call-done = bf16[1024,8192]{1,0:T(8,128)(2,1)} async-done(((bf16[1024,2048]{1,0:T(8,128)(2,1)}), bf16[1024,8192]{1,0:T(8,128)(2,1)}) %all-gather.5.cloned.1.call-update) | async-done | bytes 16777232 | tf_op jit(solution)/shard_map/all_gather | solution.py:39
  620.7 25.6 %fusion.4 = f32[4096,2048]{1,0:T(8,128)} fusion(bf16[1024,2048]{1,0:T(8,128)(2,1)} %all-gather.3.cloned.1.call-done, bf16[1024,8192]{1,0:T(8,128)(2,1)} %all-gather.5.cloned.1.call-done, s32[]{:T(128)S(6)} %select_n.31), kind=kOutput, calls=%fused_computation.4 | convolution fusion | flops 17179869184 | bytes 46137348 | tf_op jit(solution)/shard_map/dot_general | solution.py:41
  646.3 0.0 copy-start
  646.3 0.0 reduce-scatter.8.cloned.1.call-update
  646.3 120.0 %reduce-scatter.6.cloned.1.call-done = f32[512,1024]{1,0:T(8,128)} async-done(((f32[2048,1024]{1,0:T(8,128)}), f32[512,1024]{1,0:T(8,128)}) %reduce-scatter.6.cloned.1.call-update) | async-done | bytes 2097168 | tf_op jit(solution)/shard_map/reduce_scatter | solution.py:36
  766.3 0.0 copy-done
  766.3 3.3 add.25
  769.6 232.1 %reduce-scatter.8.cloned.1.call-done = f32[1024,2048]{1,0:T(8,128)} async-done(((f32[4096,2048]{1,0:T(8,128)}), f32[1024,2048]{1,0:T(8,128)}) %reduce-scatter.8.cloned.1.call-update) | async-done | bytes 8388624 | tf_op jit(solution)/shard_map/reduce_scatter | solution.py:44
  1001.7 11.9 %add.27 = f32[1024,2048]{1,0:T(8,128)} add(f32[1024,2048]{1,0:T(8,128)} %param.5, f32[1024,2048]{1,0:T(8,128)} %reduce-scatter.8.cloned.1.call-done) | non-fusion elementwise | flops 2097152 | bytes 25165824 | tf_op jit(solution)/shard_map/add | solution.py:45
Async XLA Ops:
  7.2 105.2 %reduce-scatter.4.cloned.1.call-start = ((), (), s32[]{:S(2)}) async-start(), calls=%async_computation.3 | async-start | bytes 12582912 | tf_op jit(solution)/shard_map/reduce_scatter | solution.py:20
  7.9 165.4 %all-gather.3.cloned.1.call-start = ((), (), s32[]{:S(2)}) async-start(), calls=%async_computation.4 | async-start | bytes 6291456 | tf_op jit(solution)/shard_map/all_gather | solution.py:22
  116.4 216.0 %all-reduce.3.cloned.1.call-start = ((), (), s32[]{:S(2)}) async-start(), calls=%async_computation.8 | async-start | bytes 16777216 | tf_op jit(solution)/shard_map/psum | solution.py:12
  179.4 441.4 %all-gather.5.cloned.1.call-start = ((), (), s32[]{:S(2)}) async-start(), calls=%async_computation.6 | async-start | bytes 20971520 | tf_op jit(solution)/shard_map/all_gather | solution.py:39
  179.9 586.4 %reduce-scatter.6.cloned.1.call-start = ((), (), s32[]{:S(2)}) async-start(), calls=%async_computation.5 | async-start | bytes 10485760 | tf_op jit(solution)/shard_map/reduce_scatter | solution.py:36
  347.6 654.1 %reduce-scatter.8.cloned.1.call-start = ((), (), s32[]{:S(2)}) async-start(), calls=%async_computation.7 | async-start | bytes 41943040 | tf_op jit(solution)/shard_map/reduce_scatter | solution.py:44
  646.3 120.1 %copy-start = (f32[512,1024]{1,0:T(8,128)S(1)}, f32[512,1024]{1,0:T(8,128)}, u32[]{:S(2)}) copy-start(f32[512,1024]{1,0:T(8,128)} %param.4) | copy-start | bytes 6291460
Sparse Core Ops, SparseCore 0:
  10.3 102.0 reduce-scatter.3
  116.5 56.7 all-gather.2
  179.5 152.8 all-reduce.2
  333.8 286.8 all-gather.4
  623.5 142.7 reduce-scatter.5
  768.8 232.9 reduce-scatter.7
where the time goes:
time: 1020 us
  waiting for transfers between devices  940 us (92%)
  matrix products  40.8 us (4%)
  other arithmetic  25.2 us (2%)
  between operations  14.1 us (1%)
    all_gather x1, waiting for transfers between devices, local(): whole_rows = lax.all_gather(panel, 'col', axis=1, tiled=True)  273 us
    reduce_scatter x1, waiting for transfers between devices, local(): lax.psum_scatter(right_tile, 'row', scatter_dimension=0, tiled=True)  232 us
    psum x1, waiting for transfers between devices, broadcast(): return lax.psum(kept, axis)  152 us
    reduce_scatter x1, waiting for transfers between devices, local(): lax.psum_scatter(left_tile, 'col', scatter_dimension=0, tiled=True)  120 us
    reduce_scatter x1, waiting for transfers between devices, local(): lax.psum_scatter(local_delta, 'island', scatter_dimension=0, tiled=True)  104 us
    all_gather x1, waiting for transfers between devices, local(): panel = lax.all_gather(rounded, 'island', axis=0, tiled=True)  56.8 us
    dot_general x1, matrix products, local(): lax.dot_general(right_block, panel, (((0,), (0,)), ((), ())), preferred_e...  25.6 us
  transfers between devices with their start and end apart: 6, of which 6 were waited for; matrix products, arithmetic and copies ran while one was open for 4% of the time, Pallas kernels for 0%

commit v1 on v0

--- a/solution.py
+++ b/solution.py
@@ -7,9 +7,15 @@
 N = 8192
 
 
+def add_all(x, axis):
+    blocks = lax.all_gather(x, axis, axis=0, tiled=False)
+    total = blocks.sum(axis=0)
+    return total
+
+
 def broadcast(value, axis, source):
     kept = jnp.where(lax.axis_index(axis) == source, value, 0).astype(value.dtype)
-    return lax.psum(kept, axis)
+    return add_all(kept, axis)
 
 
 def local(deltas, left_stat, right_stat):

time: 1020 us -> 1080 us (1.059)
  waiting for transfers between devices: 940 us -> 974 us
  other arithmetic: 25.2 us -> 50.9 us
    all_gather x0 -> x2, waiting for transfers between devices: none -> 199 us  [add_all(): blocks = lax.all_gather(x, axis, axis=0, tiled=False)]
    psum x1 -> x0, waiting for transfers between devices: 152 us -> none  [broadcast(): return lax.psum(kept, axis)]
    reduce_sum x0 -> x2, other arithmetic: none -> 25.6 us  [add_all(): total = blocks.sum(axis=0)]
    all_gather x1, waiting for transfers between devices: 273 us -> 259 us  [local(): whole_rows = lax.all_gather(panel, 'col', axis=1, tiled=True)]
  transfers between devices with their start and end apart: 6 -> 7, of which waited for: 6 -> 7; matrix products, arithmetic and copies ran while one was open for 4% -> 7% of each run, Pallas kernels for 0% -> 0%
where the time goes in v1:
time: 1080 us
  waiting for transfers between devices  974 us (90%)
  other arithmetic  50.9 us (5%)
  matrix products  41.8 us (4%)
  between operations  14.2 us (1%)
    all_gather x1, waiting for transfers between devices, local(): whole_rows = lax.all_gather(panel, 'col', axis=1, tiled=True)  259 us
    reduce_scatter x1, waiting for transfers between devices, local(): lax.psum_scatter(right_tile, 'row', scatter_dimension=0, tiled=True)  232 us
    all_gather x2, waiting for transfers between devices, add_all(): blocks = lax.all_gather(x, axis, axis=0, tiled=False)  199 us
    reduce_scatter x1, waiting for transfers between devices, local(): lax.psum_scatter(left_tile, 'col', scatter_dimension=0, tiled=True)  120 us
    reduce_scatter x1, waiting for transfers between devices, local(): lax.psum_scatter(local_delta, 'island', scatter_dimension=0, tiled=True)  104 us
    all_gather x1, waiting for transfers between devices, local(): panel = lax.all_gather(rounded, 'island', axis=0, tiled=True)  56.8 us
    reduce_sum x2, other arithmetic, add_all(): total = blocks.sum(axis=0)  25.6 us
    dot_general x1, matrix products, local(): lax.dot_general(right_block, panel, (((0,), (0,)), ((), ())), preferred_e...  25.5 us
  transfers between devices with their start and end apart: 7, of which 7 were waited for; matrix products, arithmetic and copies ran while one was open for 7% of the time, Pallas kernels for 0%

profile of v1, /device:TPU:0, one launch (start us, length us, event | category | flops | bytes accessed | tf_op | source)
XLA Modules:
  0.0 1080.8 jit_solution(9421333635214112867)
XLA Ops:
  7.2 0.0 reduce-scatter.4.cloned.1.call-start
  7.2 0.7 reduce-scatter.4.cloned.1.call-update
  7.9 0.0 all-gather.7.cloned.1.call-start
  7.9 104.4 %reduce-scatter.4.cloned.1.call-done = f32[512,2048]{1,0:T(8,128)} async-done(((f32[1024,2048]{1,0:T(8,128)}), f32[512,2048]{1,0:T(8,128)}) %reduce-scatter.4.cloned.1.call-update) | async-done | bytes 4194320 | tf_op jit(solution)/shard_map/reduce_scatter | solution.py:26
  112.3 4.0 multiply_convert_fusion
  116.3 0.0 all-gather.7.cloned.1.call-update
  116.4 0.0 all-gather.11.cloned.1.call-start
  116.4 56.8 %all-gather.7.cloned.1.call-done = bf16[1024,2048]{1,0:T(8,128)(2,1)} async-done(((bf16[512,2048]{1,0:T(8,128)(2,1)}), bf16[1024,2048]{1,0:T(8,128)(2,1)}) %all-gather.7.cloned.1.call-update) | async-done | bytes 4194320 | tf_op jit(solution)/shard_map/all_gather | solution.py:28
  173.2 6.1 broadcast_select_fusion.1
  179.3 0.0 all-gather.11.cloned.1.call-update
  179.3 0.0 all-gather.13.cloned.1.call-start
  179.4 0.5 all-gather.13.cloned.1.call-update
  179.9 0.0 all-gather.9.cloned.1.call-start
  180.0 0.5 all-gather.9.cloned.1.call-update
  180.5 0.0 reduce-scatter.6.cloned.1.call-start
  180.6 104.8 %all-gather.11.cloned.1.call-done = bf16[4096,2048]{1,0:T(8,128)(2,1)} async-done(((bf16[1024,2048]{1,0:T(8,128)(2,1)}), bf16[4096,2048]{1,0:T(8,128)(2,1)}) %all-gather.11.cloned.1.call-update) | async-done | bytes 16777232 | tf_op jit(solution)/shard_map/all_gather | solution.py:11
  285.4 12.8 %reduce_sum.24 = bf16[1024,2048]{1,0:T(8,128)(2,1)} reduce(bf16[4,1024,2048]{2,1,0:T(8,128)(2,1)} %bitcast.5, bf16[]{:T(256)} %constant.46.clone.1), dimensions={0}, to_apply=%region_1.2 | reduce | flops 6291456 | bytes 20971522 | tf_op jit(solution)/shard_map/reduce_sum | solution.py:12
  298.2 94.5 %all-gather.13.cloned.1.call-done = bf16[4096,2048]{1,0:T(8,128)(2,1)} async-done(((bf16[1024,2048]{1,0:T(8,128)(2,1)}), bf16[4096,2048]{1,0:T(8,128)(2,1)}) %all-gather.13.cloned.1.call-update) | async-done | bytes 16777232 | tf_op jit(solution)/shard_map/all_gather | solution.py:11
  392.8 12.8 %reduce_sum.25 = bf16[1024,2048]{1,0:T(8,128)(2,1)} reduce(bf16[4,1024,2048]{2,1,0:T(8,128)(2,1)} %bitcast.6, bf16[]{:T(256)} %constant.46.clone.1), dimensions={0}, to_apply=%region_2.3 | reduce | flops 6291456 | bytes 20971522 | tf_op jit(solution)/shard_map/reduce_sum | solution.py:12
  405.5 16.2 %fusion = f32[2048,1024]{1,0:T(8,128)} fusion(bf16[1024,2048]{1,0:T(8,128)(2,1)} %all-gather.7.cloned.1.call-done, bf16[1024,2048]{1,0:T(8,128)(2,1)} %reduce_sum.25, bf16[1024,2048]{1,0:T(8,128)(2,1)} %reduce_sum.24), kind=kOutput, calls=%fused_computation | convolution fusion | flops 8606711808 | bytes 20971520 | tf_op jit(solution)/shard_map/dot_general | solution.py:39
  421.8 0.0 reduce-scatter.6.cloned.1.call-update
  421.8 0.2 reduce-scatter.8.cloned.1.call-start
  422.0 258.9 %all-gather.9.cloned.1.call-done = bf16[1024,8192]{1,0:T(8,128)(2,1)} async-done(((bf16[1024,2048]{1,0:T(8,128)(2,1)}), bf16[1024,8192]{1,0:T(8,128)(2,1)}) %all-gather.9.cloned.1.call-update) | async-done | bytes 16777232 | tf_op jit(solution)/shard_map/all_gather | solution.py:45
  681.0 25.5 %fusion.4 = f32[4096,2048]{1,0:T(8,128)} fusion(bf16[1024,2048]{1,0:T(8,128)(2,1)} %all-gather.7.cloned.1.call-done, bf16[1024,8192]{1,0:T(8,128)(2,1)} %all-gather.9.cloned.1.call-done, s32[]{:T(128)S(6)} %select_n.31), kind=kOutput, calls=%fused_computation.4 | convolution fusion | flops 17179869184 | bytes 46137348 | tf_op jit(solution)/shard_map/dot_general | solution.py:47
  706.5 0.0 copy-start
  706.5 0.0 reduce-scatter.8.cloned.1.call-update
  706.5 120.0 %reduce-scatter.6.cloned.1.call-done = f32[512,1024]{1,0:T(8,128)} async-done(((f32[2048,1024]{1,0:T(8,128)}), f32[512,1024]{1,0:T(8,128)}) %reduce-scatter.6.cloned.1.call-update) | async-done | bytes 2097168 | tf_op jit(solution)/shard_map/reduce_scatter | solution.py:42
  826.6 0.0 copy-done
  826.6 3.3 add.21
  829.9 232.2 %reduce-scatter.8.cloned.1.call-done = f32[1024,2048]{1,0:T(8,128)} async-done(((f32[4096,2048]{1,0:T(8,128)}), f32[1024,2048]{1,0:T(8,128)}) %reduce-scatter.8.cloned.1.call-update) | async-done | bytes 8388624 | tf_op jit(solution)/shard_map/reduce_scatter | solution.py:50
  1062.1 11.9 %add.23 = f32[1024,2048]{1,0:T(8,128)} add(f32[1024,2048]{1,0:T(8,128)} %param.5, f32[1024,2048]{1,0:T(8,128)} %reduce-scatter.8.cloned.1.call-done) | non-fusion elementwise | flops 2097152 | bytes 25165824 | tf_op jit(solution)/shard_map/add | solution.py:51
Async XLA Ops:
  7.2 105.2 %reduce-scatter.4.cloned.1.call-start = ((), (), s32[]{:S(2)}) async-start(), calls=%async_computation.3 | async-start | bytes 12582912 | tf_op jit(solution)/shard_map/reduce_scatter | solution.py:26
  7.9 165.4 %all-gather.7.cloned.1.call-start = ((), (), s32[]{:S(2)}) async-start(), calls=%async_computation.4 | async-start | bytes 6291456 | tf_op jit(solution)/shard_map/all_gather | solution.py:28
  116.4 169.0 %all-gather.11.cloned.1.call-start = ((), (), s32[]{:S(2)}) async-start(), calls=%async_computation.8 | async-start | bytes 20971520 | tf_op jit(solution)/shard_map/all_gather | solution.py:11
  179.3 213.4 %all-gather.13.cloned.1.call-start = ((), (), s32[]{:S(2)}) async-start(), calls=%async_computation.9 | async-start | bytes 20971520 | tf_op jit(solution)/shard_map/all_gather | solution.py:11
  179.9 501.0 %all-gather.9.cloned.1.call-start = ((), (), s32[]{:S(2)}) async-start(), calls=%async_computation.6 | async-start | bytes 20971520 | tf_op jit(solution)/shard_map/all_gather | solution.py:45
  180.5 646.0 %reduce-scatter.6.cloned.1.call-start = ((), (), s32[]{:S(2)}) async-start(), calls=%async_computation.5 | async-start | bytes 10485760 | tf_op jit(solution)/shard_map/reduce_scatter | solution.py:42
  421.8 640.3 %reduce-scatter.8.cloned.1.call-start = ((), (), s32[]{:S(2)}) async-start(), calls=%async_computation.7 | async-start | bytes 41943040 | tf_op jit(solution)/shard_map/reduce_scatter | solution.py:50
  706.5 120.1 %copy-start = (f32[512,1024]{1,0:T(8,128)S(1)}, f32[512,1024]{1,0:T(8,128)}, u32[]{:S(2)}) copy-start(f32[512,1024]{1,0:T(8,128)} %param.4) | copy-start | bytes 6291460
Sparse Core Ops, SparseCore 0:
  10.3 102.0 reduce-scatter.3
  116.5 56.7 all-gather.6
  179.5 105.8 all-gather.10
  286.8 105.8 all-gather.12
  394.2 286.7 all-gather.8
  683.7 142.7 reduce-scatter.5
  829.1 232.9 reduce-scatter.7
